TPU v7x, 512 devices: a whole 4x4x16 slice. The times are simulated.
512 devices in a mesh: seq: 128 (over x, y_hi, z), fsdp: 4 (over y_lo, core).
Axes of the slice: x: 4, y: 4 (y_hi: 2, y_lo: 2; y = y_hi * 2 + y_lo), z: 16, core: 2. Of those that a mesh axis runs over, the one named last changes fastest.
Arguments:
- block_input: bfloat16 [8, 16384, 1536], P('fsdp', 'seq'), may hold values from -6 to 6
- dilated_weight: bfloat16 [3, 1536, 768], P(None, 'fsdp'), may hold values from -0.09375 to 0.09375
- w_project: bfloat16 [768, 1536], P('fsdp'), may hold values from -0.21875 to 0.21875
- gain_first: float32 [1536], replicated, may hold values from 0.5 to 1.5
- gain_second: float32 [768], replicated, may hold values from 0.5 to 1.5
- grad_output: bfloat16 [8, 16384, 1536], P('fsdp', 'seq'), may hold values from -6 to 6
Outputs:
- grad_input: bfloat16 [8, 16384, 1536], P('fsdp', 'seq')
- grad_gain_first: float32 [1536], replicated
- grad_gain_second: float32 [768], replicated
All inputs are finite; a program needn't handle non-finite values.
Results may differ from a plain program's by a relative error of at most 0.008.
Values may be sent and summed in bfloat16 or wider, within the bound.
No kernel may reach another device: no remote copies, remote signals or barrier semaphores. Data moves between devices by JAX's collectives and lax.ppermute only.
A program may use at most 64 MiB of HBM per device.

v0:
```python
import jax
import jax.numpy as jnp
from jax import lax
from jax.sharding import PartitionSpec as P


def shifted(value, axis, steps):
    count = lax.axis_size(axis)
    initial, last = (max(0, -steps), min(count, count - steps))
    return lax.ppermute(value, axis, [(source, source + steps) for source in range(initial, last)])


def norm_act(values, factor):
    centre = values - jnp.mean(values, axis=-1, keepdims=True)
    spread = jnp.mean(centre * centre, axis=-1, keepdims=True)
    return jax.nn.gelu(centre * lax.rsqrt(spread + 1e-05) * factor)


def far_inputs(values, amount):
    return shifted(values, "seq", amount)


def far_grads(values, amount):
    return shifted(values, "seq", amount)


def three_taps(lagging, hidden_state, leading, w_full):
    mixed_state = jnp.einsum("sbc,ch->sbh", lagging, w_full[0], preferred_element_type=jnp.float32)
    mixed_state = mixed_state + jnp.einsum(
        "sbc,ch->sbh", hidden_state, w_full[1], preferred_element_type=jnp.float32
    )
    return mixed_state + jnp.einsum(
        "sbc,ch->sbh", leading, w_full[2], preferred_element_type=jnp.float32
    )


def block_grads(
    inputs, cotangent, w_full, proj_full, gain_first, gain_second, forward_mix, taps_grad
):
    widened = inputs.astype(jnp.float32)
    hidden_state = norm_act(widened, gain_first).astype(jnp.bfloat16)
    mixed_state = forward_mix(hidden_state).astype(jnp.bfloat16)
    grad_hidden2 = jnp.einsum(
        "sbc,hc->sbh", cotangent, proj_full, preferred_element_type=jnp.float32
    )
    unused, pull_second = jax.vjp(norm_act, mixed_state.astype(jnp.float32), gain_second)
    mixed_gradient, grad_second = pull_second(grad_hidden2)
    mixed_gradient = mixed_gradient.astype(jnp.bfloat16)
    grad_ahead, grad_behind = taps_grad(mixed_gradient)
    hidden_gradient = jnp.einsum(
        "sbh,ch->sbc", grad_ahead, w_full[0], preferred_element_type=jnp.float32
    )
    hidden_gradient = hidden_gradient + jnp.einsum(
        "sbh,ch->sbc", mixed_gradient, w_full[1], preferred_element_type=jnp.float32
    )
    hidden_gradient = hidden_gradient + jnp.einsum(
        "sbh,ch->sbc", grad_behind, w_full[2], preferred_element_type=jnp.float32
    )
    unused2, pull_first = jax.vjp(norm_act, widened, gain_first)
    grad_branch, grad_first = pull_first(hidden_gradient)
    grad_local = (cotangent.astype(jnp.float32) + grad_branch).astype(jnp.bfloat16)
    return (grad_local, grad_first, grad_second)


def body(block_input, dilated_weight, w_project, gain_first, gain_second, grad_output):
    w_full, proj_full = (
        lax.all_gather(dilated_weight, "fsdp", axis=1, tiled=True),
        lax.all_gather(w_project, "fsdp", axis=0, tiled=True),
    )
    reach = lax.axis_size("seq") // 8

    def remote_mix(hidden_state):
        return three_taps(
            far_inputs(hidden_state, reach), hidden_state, far_inputs(hidden_state, -reach), w_full
        )

    def remote_grads(values):
        return (far_grads(values, -reach), far_grads(values, reach))

    grad_input, first_sum, second_sum = block_grads(
        block_input,
        grad_output,
        w_full,
        proj_full,
        gain_first,
        gain_second,
        remote_mix,
        remote_grads,
    )
    totals = lax.psum((first_sum, second_sum), ("seq", "fsdp"))
    return (grad_input, totals[0], totals[1])


def solution(mesh):
    in_specs = (
        P("fsdp", "seq", None),
        P(None, "fsdp", None),
        P("fsdp", None),
        P(),
        P(),
        P("fsdp", "seq", None),
    )
    out_specs = (P("fsdp", "seq", None), P(), P())
    return jax.shard_map(body, mesh=mesh, in_specs=in_specs, out_specs=out_specs, check_vma=False)
```

profile of v0, /device:TPU:1, one launch (start us, length us, event | category | flops | bytes accessed | tf_op | source)
XLA Modules:
  0.0 298.8 jit_solution(9477924018864004862)
XLA Ops:
  7.2 0.0 all-gather.5.cloned.1.call-start
  7.2 0.7 all-gather.5.cloned.1.call-update
  7.9 0.0 all-gather.3.cloned.1.call-start
  8.0 0.7 all-gather.3.cloned.1.call-update
  8.7 0.2 convert_reduce_fusion
  8.9 0.3 fusion.23
  9.2 0.8 fusion.19
  10.0 1.3 collective-permute-start.1
  11.3 6.3 %collective-permute-start = (bf16[2,128,1536]{2,1,0:T(8,128)(2,1)S(1)}, bf16[2,128,1536]{2,1,0:T(8,128)(2,1)S(1)}, u32[]{:S(2)}, u32[]{:S(2)}) collective-permute-start(bf16[2,128,1536]{2,1,0:T(8,128)(2,1)S(1)} %fusion.19), channel_id=1, source_target_pairs={{0,64},{4,68},{8,72},{12,76},{16,80},{20,84},{24,88},{28,92},{32,9... | collective-permute-start | bytes 2359304 | tf_op jit(solution)/shard_map/ppermute | solution.py:10
  17.7 91.2 %all-gather.5.cloned.1.call-done = bf16[3,1536,768]{2,1,0:T(8,128)(2,1)} async-done(((bf16[3,384,768]{2,1,0:T(8,128)(2,1)}), bf16[3,1536,768]{2,1,0:T(8,128)(2,1)}) %all-gather.5.cloned.1.call-update) | async-done | bytes 7077904 | tf_op jit(solution)/shard_map/all_gather | solution.py:67
  108.8 2.4 fusion.5
  111.3 0.0 collective-permute-done.1
  111.3 2.4 fusion.7
  113.7 0.0 copy-start.1
  113.8 0.0 copy-start.3
  113.8 0.0 collective-permute-done
  113.8 2.6 fusion.44
  116.4 0.2 multiply_reduce_fusion.2
  116.6 36.3 %all-gather.3.cloned.1.call-done = bf16[768,1536]{1,0:T(8,128)(2,1)} async-done(((bf16[192,1536]{1,0:T(8,128)(2,1)}), bf16[768,1536]{1,0:T(8,128)(2,1)}) %all-gather.3.cloned.1.call-update) | async-done | bytes 2359312 | tf_op jit(solution)/shard_map/all_gather | solution.py:68
  153.0 3.0 multiply_reduce_fusion.1
  156.0 0.5 multiply_reduce_fusion
  156.4 0.3 add_convert_fusion.1
  156.7 4.4 %collective-permute-start.3 = (bf16[2,128,768]{2,1,0:T(8,128)(2,1)S(1)}, bf16[2,128,768]{2,1,0:T(8,128)(2,1)S(1)}, u32[]{:S(2)}, u32[]{:S(2)}) collective-permute-start(bf16[2,128,768]{2,1,0:T(8,128)(2,1)S(1)} %add_convert_fusion.1), channel_id=1, source_target_pairs={{0,64},{4,68},{8,72},{12,76},{16,80},{20,84},{24,88},{28,92},{32,9... | collective-permute-start | bytes 1179656 | tf_op jit(solution)/shard_map/ppermute | solution.py:10
  161.1 1.3 collective-permute-start.2
  162.4 2.5 fusion.4
  164.9 13.1 %collective-permute-done.3 = bf16[2,128,768]{2,1,0:T(8,128)(2,1)S(1)} collective-permute-done((bf16[2,128,768]{2,1,0:T(8,128)(2,1)S(1)}, bf16[2,128,768]{2,1,0:T(8,128)(2,1)S(1)}, u32[]{:S(2)}, u32[]{:S(2)}) %collective-permute-start.3) | collective-permute-done | bytes 393248 | tf_op jit(solution)/shard_map/ppermute | solution.py:10
  178.0 2.5 fusion.6
  180.5 0.0 collective-permute-done.2
  180.5 3.7 %fusion.24 = (f32[2,128]{1,0:T(2,128)S(1)}, f32[2,128,1536]{2,1,0:T(8,128)S(1)}) fusion(bf16[2,128,1536]{2,1,0:T(8,128)(2,1)S(1)} %copy-done, f32[1536]{0:T(1024)S(1)} %copy-done.2, f32[2,128]{1,0:T(2,128)S(1)} %broadcast_multiply_fusion.1, f32[2,128]{1,0:T(2,128)S(1)} %fusion.42, f32[2,128,1536]{2,1,0:T(8,128)S(1)} %fusion.6, ...), kind=kOutput, calls=%fused_computation.33 | convolution fusion | flops 614989568 | bytes 8266752 | tf_op jit(solution)/shard_map/sbh,ch->sbc/dot_general | solution.py:50
  184.2 0.7 fusion.22
  185.0 1.5 add_convert_fusion
  186.5 105.5 %all-reduce = (f32[1536]{0:T(1024)}, f32[768]{0:T(1024)}) all-reduce(f32[1536]{0:T(1024)S(1)} %get-tuple-element.3, f32[768]{0:T(1024)S(1)} %get-tuple-element.5), channel_id=1, replica_groups=mesh['seq'=128,'fsdp'=4] {'seq','fsdp'}, use_global_device_ids=true, to_apply=%region_9.0 | all-reduce | flops 2304 | bytes 18432 | tf_op jit(solution)/shard_map/psum | solution.py:90
  (14 shorter events, 0.1 us)
Async XLA Ops:
  7.2 1.5 copy-start
  7.2 2.1 copy-start.2
  7.2 101.7 %all-gather.5.cloned.1.call-start = ((), (), s32[]{:S(2)}) async-start(), calls=%async_computation.1 | async-start | bytes 8847360 | tf_op jit(solution)/shard_map/all_gather | solution.py:67
  7.9 145.0 %all-gather.3.cloned.1.call-start = ((), (), s32[]{:S(2)}) async-start(), calls=%async_computation | async-start | bytes 2949120 | tf_op jit(solution)/shard_map/all_gather | solution.py:68
  10.0 101.3 %collective-permute-start.1 = (bf16[2,128,1536]{2,1,0:T(8,128)(2,1)S(1)}, bf16[2,128,1536]{2,1,0:T(8,128)(2,1)S(1)}, u32[]{:S(2)}, u32[]{:S(2)}) collective-permute-start(bf16[2,128,1536]{2,1,0:T(8,128)(2,1)S(1)} %fusion.19), channel_id=1, source_target_pairs={{64,0},{68,4},{72,8},{76,12},{80,16},{84,20},{88,24},{92,28},{96,3... | collective-permute-start | bytes 2359304 | tf_op jit(solution)/shard_map/ppermute | solution.py:10
  11.3 102.4 %collective-permute-start = (bf16[2,128,1536]{2,1,0:T(8,128)(2,1)S(1)}, bf16[2,128,1536]{2,1,0:T(8,128)(2,1)S(1)}, u32[]{:S(2)}, u32[]{:S(2)}) collective-permute-start(bf16[2,128,1536]{2,1,0:T(8,128)(2,1)S(1)} %fusion.19), channel_id=1, source_target_pairs={{0,64},{4,68},{8,72},{12,76},{16,80},{20,84},{24,88},{28,92},{32,9... | collective-permute-start | bytes 2359304 | tf_op jit(solution)/shard_map/ppermute | solution.py:10
  113.7 39.2 %copy-start.1 = (bf16[2,128,1536]{2,1,0:T(8,128)(2,1)S(1)}, bf16[2,128,1536]{2,1,0:T(8,128)(2,1)}, u32[]{:S(2)}) copy-start(bf16[2,128,1536]{2,1,0:T(8,128)(2,1)} %param.11) | copy-start | bytes 2359300
  113.8 39.2 %copy-start.3 = (f32[768]{0:T(1024)S(1)}, f32[768]{0:T(1024)}, u32[]{:S(2)}) copy-start(f32[768]{0:T(1024)} %param.10) | copy-start | bytes 9220
  156.7 21.3 %collective-permute-start.3 = (bf16[2,128,768]{2,1,0:T(8,128)(2,1)S(1)}, bf16[2,128,768]{2,1,0:T(8,128)(2,1)S(1)}, u32[]{:S(2)}, u32[]{:S(2)}) collective-permute-start(bf16[2,128,768]{2,1,0:T(8,128)(2,1)S(1)} %add_convert_fusion.1), channel_id=1, source_target_pairs={{0,64},{4,68},{8,72},{12,76},{16,80},{20,84},{24,88},{28,92},{32,9... | collective-permute-start | bytes 1179656 | tf_op jit(solution)/shard_map/ppermute | solution.py:10
  161.1 19.4 %collective-permute-start.2 = (bf16[2,128,768]{2,1,0:T(8,128)(2,1)S(1)}, bf16[2,128,768]{2,1,0:T(8,128)(2,1)S(1)}, u32[]{:S(2)}, u32[]{:S(2)}) collective-permute-start(bf16[2,128,768]{2,1,0:T(8,128)(2,1)S(1)} %add_convert_fusion.1), channel_id=1, source_target_pairs={{64,0},{68,4},{72,8},{76,12},{80,16},{84,20},{88,24},{92,28},{96,3... | collective-permute-start | bytes 1179656 | tf_op jit(solution)/shard_map/ppermute | solution.py:10
Sparse Core Ops, SparseCore 0:
  10.1 98.6 all-gather.4
  110.9 41.9 all-gather.2
where the time goes:
time: 299 us
  waiting for transfers between devices  142 us (47%)
  blocking collectives  106 us (35%)
  matrix products  19.1 us (6%)
  between operations  14.2 us (5%)
  starting transfers between devices  13.4 us (4%)
  other arithmetic  4.61 us (2%)
    psum x1, blocking collectives, body(): totals = lax.psum((first_sum, second_sum), ('seq', 'fsdp'))  106 us
    all_gather x1, waiting for transfers between devices, body(): lax.all_gather(dilated_weight, 'fsdp', axis=1, tiled=True)  91.2 us
    all_gather x1, waiting for transfers between devices, body(): lax.all_gather(w_project, 'fsdp', axis=0, tiled=True)  36.3 us
    ppermute x4, starting transfers between devices, shifted(): lax.ppermute(value, axis, [(source, source + steps) for source in range(i...  13.3 us
    ppermute x4, waiting for transfers between devices, shifted(): lax.ppermute(value, axis, [(source, source + steps) for source in range(i...  13.1 us
  transfers between devices with their start and end apart: 6, of which 3 were waited for; matrix products, arithmetic and copies ran while one was open for 5% of the time, Pallas kernels for 0%

commit v1 on v0

--- a/solution.py
+++ b/solution.py
@@ -87,7 +87,7 @@
         remote_mix,
         remote_grads,
     )
-    totals = lax.psum((first_sum, second_sum), ("seq", "fsdp"))
+    totals = lax.psum(lax.psum((first_sum, second_sum), "seq"), "fsdp")
     return (grad_input, totals[0], totals[1])
 
 

time: 299 us -> 908 us (3.04)
  blocking collectives: 106 us -> 715 us
    psum x1 -> x2, blocking collectives: 106 us -> 715 us  [body(): totals = lax.psum(lax.psum((first_sum, second_sum), 'seq'), 'fsdp')]
  transfers between devices with their start and end apart: 6 -> 6, of which waited for: 3 -> 3; matrix products, arithmetic and copies ran while one was open for 5% -> 2% of each run, Pallas kernels for 0% -> 0%
where the time goes in v1:
time: 908 us
  blocking collectives  715 us (79%)
  waiting for transfers between devices  142 us (16%)
  matrix products  19.1 us (2%)
  between operations  14.2 us (2%)
  starting transfers between devices  13.4 us (1%)
    psum x2, blocking collectives, body(): totals = lax.psum(lax.psum((first_sum, second_sum), 'seq'), 'fsdp')  715 us
    all_gather x1, waiting for transfers between devices, body(): lax.all_gather(dilated_weight, 'fsdp', axis=1, tiled=True)  91.2 us
    all_gather x1, waiting for transfers between devices, body(): lax.all_gather(w_project, 'fsdp', axis=0, tiled=True)  36.3 us
  transfers between devices with their start and end apart: 6, of which 3 were waited for; matrix products, arithmetic and copies ran while one was open for 2% of the time, Pallas kernels for 0%

profile of v1, /device:TPU:1, one launch (start us, length us, event | category | flops | bytes accessed | tf_op | source)
XLA Modules:
  0.0 907.9 jit_solution(16876836173069426962)
XLA Ops:
  7.2 0.0 all-gather.5.cloned.1.call-start
  7.2 0.7 all-gather.5.cloned.1.call-update
  7.9 0.0 all-gather.3.cloned.1.call-start
  8.0 0.7 all-gather.3.cloned.1.call-update
  8.7 0.2 convert_reduce_fusion
  8.9 0.3 fusion.23
  9.2 0.8 fusion.19
  10.0 1.3 collective-permute-start.1
  11.3 6.3 collective-permute-start
  17.7 91.2 %all-gather.5.cloned.1.call-done = bf16[3,1536,768]{2,1,0:T(8,128)(2,1)} async-done(((bf16[3,384,768]{2,1,0:T(8,128)(2,1)}), bf16[3,1536,768]{2,1,0:T(8,128)(2,1)}) %all-gather.5.cloned.1.call-update) | async-done | bytes 7077904 | tf_op jit(solution)/shard_map/all_gather | solution.py:67
  108.8 2.4 fusion.5
  111.3 2.4 fusion.7
  113.7 0.0 copy-start.1
  113.8 0.0 copy-start.3
  113.8 0.0 collective-permute-done
  113.8 2.6 fusion.44
  116.4 0.2 multiply_reduce_fusion.2
  116.6 36.3 %all-gather.3.cloned.1.call-done = bf16[768,1536]{1,0:T(8,128)(2,1)} async-done(((bf16[192,1536]{1,0:T(8,128)(2,1)}), bf16[768,1536]{1,0:T(8,128)(2,1)}) %all-gather.3.cloned.1.call-update) | async-done | bytes 2359312 | tf_op jit(solution)/shard_map/all_gather | solution.py:68
  153.0 3.0 multiply_reduce_fusion.1
  156.0 0.5 multiply_reduce_fusion
  156.4 0.3 add_convert_fusion.1
  156.7 4.4 collective-permute-start.3
  161.1 1.3 collective-permute-start.2
  162.4 2.5 fusion.4
  164.9 13.1 %collective-permute-done.3 = bf16[2,128,768]{2,1,0:T(8,128)(2,1)S(1)} collective-permute-done((bf16[2,128,768]{2,1,0:T(8,128)(2,1)S(1)}, bf16[2,128,768]{2,1,0:T(8,128)(2,1)S(1)}, u32[]{:S(2)}, u32[]{:S(2)}) %collective-permute-start.3) | collective-permute-done | bytes 393248 | tf_op jit(solution)/shard_map/ppermute | solution.py:10
  178.0 2.5 fusion.6
  180.5 0.0 collective-permute-done.2
  180.5 3.7 fusion.24
  184.2 0.7 fusion.22
  185.0 1.5 add_convert_fusion
  186.5 594.7 %all-reduce = (f32[1536]{0:T(1024)S(1)}, f32[768]{0:T(1024)S(1)}) all-reduce(f32[1536]{0:T(1024)S(1)} %get-tuple-element.3, f32[768]{0:T(1024)S(1)} %get-tuple-element.5), channel_id=1, replica_groups=mesh['seq'=128,'fsdp'=4] {'seq'}, use_global_device_ids=true, to_apply=%region_9.0 | all-reduce | flops 2304 | bytes 18432 | tf_op jit(solution)/shard_map/psum | solution.py:90
  781.2 119.8 %all-reduce.1 = (f32[1536]{0:T(1024)}, f32[768]{0:T(1024)}) all-reduce(f32[1536]{0:T(1024)S(1)} %get-tuple-element.7, f32[768]{0:T(1024)S(1)} %get-tuple-element.8), channel_id=1, replica_groups=mesh['seq'=128,'fsdp'=4] {'fsdp'}, use_global_device_ids=true, to_apply=%region_10.0 | all-reduce | flops 2304 | bytes 18432 | tf_op jit(solution)/shard_map/psum | solution.py:90
  (15 shorter events, 0.1 us)
Async XLA Ops:
  7.2 1.5 copy-start
  7.2 2.1 copy-start.2
  7.2 101.7 %all-gather.5.cloned.1.call-start = ((), (), s32[]{:S(2)}) async-start(), calls=%async_computation.1 | async-start | bytes 8847360 | tf_op jit(solution)/shard_map/all_gather | solution.py:67
  7.9 145.0 %all-gather.3.cloned.1.call-start = ((), (), s32[]{:S(2)}) async-start(), calls=%async_computation | async-start | bytes 2949120 | tf_op jit(solution)/shard_map/all_gather | solution.py:68
  10.0 101.3 %collective-permute-start.1 = (bf16[2,128,1536]{2,1,0:T(8,128)(2,1)S(1)}, bf16[2,128,1536]{2,1,0:T(8,128)(2,1)S(1)}, u32[]{:S(2)}, u32[]{:S(2)}) collective-permute-start(bf16[2,128,1536]{2,1,0:T(8,128)(2,1)S(1)} %fusion.19), channel_id=1, source_target_pairs={{64,0},{68,4},{72,8},{76,12},{80,16},{84,20},{88,24},{92,28},{96,3... | collective-permute-start | bytes 2359304 | tf_op jit(solution)/shard_map/ppermute | solution.py:10
  11.3 102.4 %collective-permute-start = (bf16[2,128,1536]{2,1,0:T(8,128)(2,1)S(1)}, bf16[2,128,1536]{2,1,0:T(8,128)(2,1)S(1)}, u32[]{:S(2)}, u32[]{:S(2)}) collective-permute-start(bf16[2,128,1536]{2,1,0:T(8,128)(2,1)S(1)} %fusion.19), channel_id=1, source_target_pairs={{0,64},{4,68},{8,72},{12,76},{16,80},{20,84},{24,88},{28,92},{32,9... | collective-permute-start | bytes 2359304 | tf_op jit(solution)/shard_map/ppermute | solution.py:10
  113.7 39.2 %copy-start.1 = (bf16[2,128,1536]{2,1,0:T(8,128)(2,1)S(1)}, bf16[2,128,1536]{2,1,0:T(8,128)(2,1)}, u32[]{:S(2)}) copy-start(bf16[2,128,1536]{2,1,0:T(8,128)(2,1)} %param.11) | copy-start | bytes 2359300
  113.8 39.2 %copy-start.3 = (f32[768]{0:T(1024)S(1)}, f32[768]{0:T(1024)}, u32[]{:S(2)}) copy-start(f32[768]{0:T(1024)} %param.10) | copy-start | bytes 9220
  156.7 21.3 %collective-permute-start.3 = (bf16[2,128,768]{2,1,0:T(8,128)(2,1)S(1)}, bf16[2,128,768]{2,1,0:T(8,128)(2,1)S(1)}, u32[]{:S(2)}, u32[]{:S(2)}) collective-permute-start(bf16[2,128,768]{2,1,0:T(8,128)(2,1)S(1)} %add_convert_fusion.1), channel_id=1, source_target_pairs={{0,64},{4,68},{8,72},{12,76},{16,80},{20,84},{24,88},{28,92},{32,9... | collective-permute-start | bytes 1179656 | tf_op jit(solution)/shard_map/ppermute | solution.py:10
  161.1 19.4 %collective-permute-start.2 = (bf16[2,128,768]{2,1,0:T(8,128)(2,1)S(1)}, bf16[2,128,768]{2,1,0:T(8,128)(2,1)S(1)}, u32[]{:S(2)}, u32[]{:S(2)}) collective-permute-start(bf16[2,128,768]{2,1,0:T(8,128)(2,1)S(1)} %add_convert_fusion.1), channel_id=1, source_target_pairs={{64,0},{68,4},{72,8},{76,12},{80,16},{84,20},{88,24},{92,28},{96,3... | collective-permute-start | bytes 1179656 | tf_op jit(solution)/shard_map/ppermute | solution.py:10
Sparse Core Ops, SparseCore 0:
  10.1 98.6 all-gather.4
  110.9 41.9 all-gather.2
